TPU v7x, 32 devices: a whole 2x2x4 slice. The times are simulated.
32 devices in a mesh: tiles: 8 (over z, x), lev: 4 (over y, core).
Axes of the slice: x: 2, y: 2, z: 4, core: 2. Of those that a mesh axis runs over, the one named last changes fastest.
Arguments:
- land_smb: bfloat16 [512, 10, 128], P(('tiles', 'lev')), may hold values from -6 to 6
- block_weights: bfloat16 [1024, 128, 1024], P(('tiles', 'lev')), may hold values from -0.5 to 0.5
- block_tile: int32 [1024], P(('tiles', 'lev')), may hold values from 0 to 255, as said below
- block_land: int32 [1024], P(('tiles', 'lev')), may hold values from 0 to 15
- block_class: int32 [1024], P(('tiles', 'lev')), may hold values from 0 to 9
- ice_mask: int32 [64, 4096], P('tiles', 'lev'), may hold values 0 or 1
- thickness: float32 [64, 4096], P('tiles', 'lev'), may hold values from 0.5 to 2
- prev_smb: float32 [64, 4096], P('tiles', 'lev'), may hold values from -6 to 6
- basal_friction: float32 [64, 4096], P('tiles', 'lev'), may hold values from 0.05 to 0.5
- driving: float32 [10, 64, 4096], P(None, 'tiles', 'lev'), may hold values from -54 to 54
- velocity_start: float32 [10, 64, 4096], P(None, 'tiles', 'lev'), may hold values from -6 to 6
Outputs:
- ice_smb: float32 [64, 4096], P('tiles')
- velocity_end: float32 [10, 64, 4096], P(None, 'tiles', 'lev')
Inputs may be any that keep to these rules, and one draw needn't show every extreme that they name: `block_tile`: ice tile t lies on index t // 32 of tiles. Of the 32 remap blocks of one device, at most 8 name tiles on any one index of tiles; in every draw some index of tiles receives exactly 8 from every device.
All inputs are finite; a program needn't handle non-finite values. No bound on the sum of `ice_mask` on one device may be relied on, other than what follows from the above.
Results may differ from a plain program's by a relative error of at most 0.0003.
Values sent between devices are 32-bit elements; how exact they have to be, the bound alone decides.
A program may use at most 64 MiB of HBM per device.

v0:
```python
import jax
import jax.numpy as jnp
from jax import lax
from jax.sharding import PartitionSpec as P

CX = 8
TW = 128
TPD = 32
ITERS = 4
VISC_FLOOR = 0.25
VERTICAL = 4.0
SMB_WEIGHT = 0.5


def extended(cells, sides, width):
    for axis, dim in sides:
        count = lax.axis_size(axis)
        ends = count - 1
        head = lax.slice_in_dim(cells, 0, width, axis=dim)
        tail = lax.slice_in_dim(cells, cells.shape[dim] - width, cells.shape[dim], axis=dim)
        cells = jnp.concatenate(
            [
                lax.ppermute(tail, axis, [(i, (i + 1) % count) for i in range(ends)]),
                cells,
                lax.ppermute(head, axis, [((i + 1) % count, i) for i in range(ends)]),
            ],
            axis=dim,
        )
    return cells


def visc_from(box, ice_frac):
    slope_x = (box[:, 2:, 1:-1] - box[:, :-2, 1:-1]) * 0.5
    slope_y = (box[:, 1:-1, 2:] - box[:, 1:-1, :-2]) * 0.5
    return ice_frac * (VISC_FLOOR + slope_x * slope_x + slope_y * slope_y) ** (-1.0 / 3.0)


def level_pad(box):
    return jnp.pad(box, ((1, 1), (0, 0), (0, 0)))


def face_weights(visc_box, drag):
    center = visc_box[1:-1, 1:-1, 1:-1]
    east_face = jnp.sqrt(center * visc_box[1:-1, 2:, 1:-1])
    west_face = jnp.sqrt(center * visc_box[1:-1, :-2, 1:-1])
    north_face = jnp.sqrt(center * visc_box[1:-1, 1:-1, 2:])
    south_face = jnp.sqrt(center * visc_box[1:-1, 1:-1, :-2])
    upper_face = VERTICAL * jnp.sqrt(center * visc_box[2:, 1:-1, 1:-1])
    lower_face = VERTICAL * jnp.sqrt(center * visc_box[:-2, 1:-1, 1:-1])
    diagonal_sum = drag + east_face + west_face + north_face + south_face + upper_face + lower_face
    return (diagonal_sum, east_face, west_face, upper_face, lower_face, north_face, south_face)


def apply_operator(faces, field_box):
    diagonal_sum, east_face, west_face, upper_face, lower_face, north_face, south_face = faces
    center = field_box[1:-1, 1:-1, 1:-1]
    result = (
        diagonal_sum * center
        - east_face * field_box[1:-1, 2:, 1:-1]
        - west_face * field_box[1:-1, :-2, 1:-1]
    )
    result = (
        result - upper_face * field_box[2:, 1:-1, 1:-1] - lower_face * field_box[:-2, 1:-1, 1:-1]
    )
    return result - north_face * field_box[1:-1, 1:-1, 2:] - south_face * field_box[1:-1, 1:-1, :-2]


def apply_local(faces, field):
    field_box = extended(field, (("tiles", 1), ("lev", 2)), 1)
    return apply_operator(faces, level_pad(field_box))


def paired_totals(residual, image):
    return lax.psum((jnp.sum(residual * residual), jnp.sum(residual * image)), ("tiles", "lev"))


def krylov_merged(faces, rhs, start):
    solution = start
    residual = rhs - apply_local(faces, start)
    image = apply_local(faces, residual)
    norm_now, product = paired_totals(residual, image)
    step_len = norm_now / product
    direction = residual
    along = image
    for iteration in range(ITERS):
        solution = solution + step_len * direction
        residual = residual - step_len * along
        if iteration + 1 < ITERS:
            image = apply_local(faces, residual)
            norm_next, product = paired_totals(residual, image)
            ratio = norm_next / norm_now
            step_len = norm_next / (product - ratio * norm_next / step_len)
            direction = residual + ratio * direction
            along = image + ratio * along
            norm_now = norm_next
    return solution


def sent_visc(velocity, ice_frac):
    x_box = extended(velocity, (("tiles", 1), ("lev", 2)), 1)
    viscosity = visc_from(x_box, ice_frac)
    visc_box = extended(viscosity, (("tiles", 1), ("lev", 2)), 1)
    return level_pad(visc_box)


def body(
    land_smb,
    block_weights,
    block_tile,
    block_land,
    block_class,
    ice_mask,
    thickness,
    prev_smb,
    basal_friction,
    driving,
    velocity_start,
):
    local_blocks, classes, land_cols = land_smb.shape
    blocks_here = block_tile.shape[0]
    tile_cells = block_weights.shape[2]
    land_rows = land_smb.reshape(local_blocks * classes, land_cols)
    picked = land_rows[block_land * classes + block_class]
    products = jnp.einsum("bl,blt->bt", picked, block_weights, preferred_element_type=jnp.float32)
    owners = lax.axis_size("tiles")
    capacity = max(2, 2 * blocks_here // owners)
    destination = block_tile // TPD
    local_tile = block_tile % TPD
    positions = jnp.arange(blocks_here, dtype=jnp.int32)
    earlier = jnp.logical_and(
        destination[None, :] == destination[:, None], positions[None, :] < positions[:, None]
    )
    ranks = jnp.sum(earlier.astype(jnp.int32), axis=1)
    slots = destination * capacity + ranks
    slot_ids = jnp.arange(owners * capacity, dtype=jnp.int32)
    slot_match = slots[None, :] == slot_ids[:, None]
    slot_hot = slot_match.astype(jnp.float32)
    sending = jnp.dot(
        slot_hot, products, precision=lax.Precision.HIGHEST, preferred_element_type=jnp.float32
    )
    sending = sending.reshape(owners, capacity, tile_cells)
    slot_tile = jnp.sum(jnp.where(slot_match, (local_tile + 1)[None, :], 0), axis=1) - 1
    slot_tile = slot_tile.reshape(owners, capacity)
    received, recv_tile = (
        lax.all_to_all(sending, "tiles", split_axis=0, concat_axis=0, tiled=True),
        lax.all_to_all(slot_tile, "tiles", split_axis=0, concat_axis=0, tiled=True),
    )
    tile_hot = (recv_tile.reshape(-1)[None, :] == jnp.arange(TPD, dtype=jnp.int32)[:, None]).astype(
        jnp.float32
    )
    partial_sums = jnp.dot(
        tile_hot,
        received.reshape(-1, tile_cells),
        precision=lax.Precision.HIGHEST,
        preferred_element_type=jnp.float32,
    )
    totals = lax.psum(partial_sums, "lev")
    ice_smb = totals.reshape(TPD, CX, TW).transpose(1, 0, 2).reshape(CX, TPD * TW)
    ice_frac = ice_mask.astype(jnp.float32)
    rhs = (ice_frac * (thickness + SMB_WEIGHT * prev_smb))[None] * driving
    drag = (ice_frac * basal_friction + (1.0 - ice_frac))[None]
    velocity = velocity_start
    visc_box = sent_visc(velocity, ice_frac[None])
    faces = face_weights(visc_box, drag)
    velocity = krylov_merged(faces, rhs, velocity)
    return (ice_smb, velocity)


def solution(mesh):
    in_specs = (
        P(("tiles", "lev"), None, None),
        P(("tiles", "lev"), None, None),
        P(("tiles", "lev")),
        P(("tiles", "lev")),
        P(("tiles", "lev")),
        P("tiles", "lev"),
        P("tiles", "lev"),
        P("tiles", "lev"),
        P("tiles", "lev"),
        P(None, "tiles", "lev"),
        P(None, "tiles", "lev"),
    )
    out_specs = (P("tiles", None), P(None, "tiles", "lev"))
    return jax.shard_map(body, mesh=mesh, in_specs=in_specs, out_specs=out_specs, check_vma=False)
```

profile of v0, /device:TPU:0, one launch (start us, length us, event | category | flops | bytes accessed | tf_op | source)
XLA Modules:
  0.0 379.7 jit_solution(6685467221838924000)
XLA Ops:
  8.3 1.3 collective-permute-start
  9.6 5.5 %collective-permute-start.1 = (f32[10,1,1024]{2,1,0:T(1,128)S(1)}, f32[10,1,1024]{2,1,0:T(1,128)S(1)}, u32[]{:S(2)}, u32[]{:S(2)}) collective-permute-start(f32[10,1,1024]{2,1,0:T(1,128)S(1)} %get-tuple-element.46), channel_id=1, source_target_pairs={{0,4},{4,8},{8,12},{12,16},{16,20},{20,24},{24,28},{1,5},{5,9},{9,... | collective-permute-start | bytes 122888 | tf_op jit(solution)/shard_map/ppermute | solution.py:23
  15.2 1.6 collective-permute-done.1
  18.0 1.3 collective-permute-start.2
  19.3 3.0 collective-permute-start.3
  22.3 1.4 add_multiply_fusion
  24.5 2.2 power_multiply_fusion
  26.8 1.3 collective-permute-start.4
  28.1 5.4 %collective-permute-start.5 = (f32[10,1,1024]{2,1,0:T(1,128)S(1)}, f32[10,1,1024]{2,1,0:T(1,128)S(1)}, u32[]{:S(2)}, u32[]{:S(2)}) collective-permute-start(f32[10,1,1024]{2,1,0:T(1,128)S(1)} %get-tuple-element.44), channel_id=1, source_target_pairs={{0,4},{4,8},{8,12},{12,16},{16,20},{20,24},{24,28},{1,5},{5,9},{9,... | collective-permute-start | bytes 122888 | tf_op jit(solution)/shard_map/ppermute | solution.py:23
  35.9 1.3 collective-permute-start.6
  37.2 3.0 collective-permute-start.7
  42.0 3.4 fusion.11
  45.5 1.3 collective-permute-start.8
  46.8 5.4 %collective-permute-start.9 = (f32[10,1,1024]{2,1,0:T(1,128)S(1)}, f32[10,1,1024]{2,1,0:T(1,128)S(1)}, u32[]{:S(2)}, u32[]{:S(2)}) collective-permute-start(f32[10,1,1024]{2,1,0:T(1,128)S(1)} %get-tuple-element.42), channel_id=1, source_target_pairs={{0,4},{4,8},{8,12},{12,16},{16,20},{20,24},{24,28},{1,5},{5,9},{9,... | collective-permute-start | bytes 122888 | tf_op jit(solution)/shard_map/ppermute | solution.py:23
  54.1 3.5 collective-permute-start.10
  57.6 1.3 collective-permute-start.11
  59.6 3.9 %collective-permute-done.11 = f32[10,10,1]{2,1,0:T(8,128)S(1)} collective-permute-done((f32[10,10,1]{2,1,0:T(8,128)S(1)}, f32[10,10,1]{2,1,0:T(8,128)S(1)}, u32[]{:S(2)}, u32[]{:S(2)}) %collective-permute-start.11) | collective-permute-done | bytes 432 | tf_op jit(solution)/shard_map/ppermute | solution.py:25
  64.6 3.3 multiply_reduce_fusion.5
  67.9 45.4 %all-reduce.9 = (f32[]{:T(128)}, f32[]{:T(128)}) all-reduce(f32[]{:T(128)} %get-tuple-element.7, f32[]{:T(128)} %get-tuple-element.6), channel_id=1, replica_groups=mesh['tiles'=8,'lev'=4] {'tiles','lev'}, use_global_device_ids=true, to_apply=%region_4.5 | all-reduce | flops 2 | bytes 16 | tf_op jit(solution)/shard_map/psum | solution.py:74
  114.6 1.3 collective-permute-start.12
  115.9 4.8 %collective-permute-start.13 = (f32[10,1,1024]{2,1,0:T(1,128)S(1)}, f32[10,1,1024]{2,1,0:T(1,128)S(1)}, u32[]{:S(2)}, u32[]{:S(2)}) collective-permute-start(f32[10,1,1024]{2,1,0:T(1,128)S(1)} %get-tuple-element.40), channel_id=1, source_target_pairs={{0,4},{4,8},{8,12},{12,16},{16,20},{20,24},{24,28},{1,5},{5,9},{9,... | collective-permute-start | bytes 122888 | tf_op jit(solution)/shard_map/ppermute | solution.py:23
  121.4 5.9 %all-to-all-start = ((s32[8,1,8]{2,1,0:T(1,128)}), s32[8,1,8]{2,1,0:T(1,128)}, u32[]{:S(2)}, u32[]{:S(2)}) async-start(s32[8,1,8]{2,1,0:T(1,128)} %bitcast), calls=%async_computation | async-start | bytes 8192 | tf_op jit(solution)/shard_map/all_to_all | solution.py:146
  127.6 1.3 collective-permute-start.14
  128.9 1.3 collective-permute-start.15
  131.4 3.0 collective-permute-done.15
  135.6 3.3 multiply_reduce_fusion.3
  138.8 42.6 %all-reduce.8 = (f32[]{:T(128)}, f32[]{:T(128)}) all-reduce(f32[]{:T(128)} %get-tuple-element.5, f32[]{:T(128)} %get-tuple-element.4), channel_id=1, replica_groups=mesh['tiles'=8,'lev'=4] {'tiles','lev'}, use_global_device_ids=true, to_apply=%region_8.9 | all-reduce | flops 2 | bytes 16 | tf_op jit(solution)/shard_map/psum | solution.py:74
  186.2 1.3 collective-permute-start.16
  187.5 4.8 %collective-permute-start.17 = (f32[10,1,1024]{2,1,0:T(1,128)S(1)}, f32[10,1,1024]{2,1,0:T(1,128)S(1)}, u32[]{:S(2)}, u32[]{:S(2)}) collective-permute-start(f32[10,1,1024]{2,1,0:T(1,128)S(1)} %get-tuple-element.38), channel_id=1, source_target_pairs={{0,4},{4,8},{8,12},{12,16},{16,20},{20,24},{24,28},{1,5},{5,9},{9,... | collective-permute-start | bytes 122888 | tf_op jit(solution)/shard_map/ppermute | solution.py:23
  196.5 1.3 collective-permute-start.18
  197.8 1.5 collective-permute-start.19
  199.2 5.2 %fusion.74 = f32[32,1,1024]{2,1,0:T(1,128)} fusion(bf16[32,128,1024]{2,1,0:T(8,128)(2,1)} %param.12, bf16[32,128,1]{1,0,2:T(8,128)(2,1)S(1)} %bitcast.19), kind=kOutput, calls=%fused_computation.159 | convolution fusion | flops 8388608 | bytes 8527872 | tf_op jit(solution)/shard_map/bl,blt->bt/dot_general | solution.py:124
  204.5 2.3 concatenate.141
  206.8 4.0 %multiply_reduce_fusion.1 = (f32[]{:T(128)}, f32[]{:T(128)}, f32[10,8,1024]{2,1,0:T(8,128)}) fusion(f32[10,8,1024]{2,1,0:T(8,128)S(1)} %multiply_subtract_fusion.1, f32[10,1,1024]{2,1,0:T(1,128)S(1)} %collective-permute-done.16, f32[10,1,1024]{2,1,0:T(1,128)S(1)} %collective-permute-done.17, f32[10,10,1]{2,1,0:T(8,128)S(1)} %collective-permute-done.18, ...), kind=kLoop, calls=%fused_computation.142 | loop fusion | flops 3522558 | bytes 2247016 | tf_op jit(solution)/shard_map/reduce_sum | solution.py:74
  210.8 44.5 %all-reduce.7 = (f32[]{:T(128)}, f32[]{:T(128)}) all-reduce(f32[]{:T(128)} %get-tuple-element.3, f32[]{:T(128)} %get-tuple-element.2), channel_id=1, replica_groups=mesh['tiles'=8,'lev'=4] {'tiles','lev'}, use_global_device_ids=true, to_apply=%region_12.13 | all-reduce | flops 2 | bytes 16 | tf_op jit(solution)/shard_map/psum | solution.py:74
  259.1 1.8 multiply_reduce_fusion
  260.9 1.3 collective-permute-start.20
  262.2 4.8 %collective-permute-start.21 = (f32[10,1,1024]{2,1,0:T(1,128)S(1)}, f32[10,1,1024]{2,1,0:T(1,128)S(1)}, u32[]{:S(2)}, u32[]{:S(2)}) collective-permute-start(f32[10,1,1024]{2,1,0:T(1,128)S(1)} %get-tuple-element.36), channel_id=1, source_target_pairs={{0,4},{4,8},{8,12},{12,16},{16,20},{20,24},{24,28},{1,5},{5,9},{9,... | collective-permute-start | bytes 122888 | tf_op jit(solution)/shard_map/ppermute | solution.py:23
  267.0 2.0 convolution_bitcast_fusion
  270.3 6.3 %all-to-all-start.1 = ((f32[8,8,1024]{2,1,0:T(8,128)}), f32[8,8,1024]{2,1,0:T(8,128)}, u32[]{:S(2)}, u32[]{:S(2)}) async-start(f32[8,8,1024]{2,1,0:T(8,128)} %convolution_bitcast_fusion), calls=%async_computation.1 | async-start | bytes 524288 | tf_op jit(solution)/shard_map/all_to_all | solution.py:145
  277.4 1.9 collective-permute-start.22
  281.1 1.9 reduce.3
  283.0 1.3 eq.49
  284.7 2.1 concatenate.147
  286.8 3.4 fusion.70
  290.2 43.7 %all-reduce.6 = (f32[]{:T(128)}, f32[]{:T(128)}) all-reduce(f32[]{:T(128)} %get-tuple-element.16, f32[]{:T(128)} %fusion.70), channel_id=1, replica_groups=mesh['tiles'=8,'lev'=4] {'tiles','lev'}, use_global_device_ids=true, to_apply=%region_16.17 | all-reduce | flops 2 | bytes 16 | tf_op jit(solution)/shard_map/psum | solution.py:74
  340.2 31.1 %all-reduce.12.cloned.1.call-done = f32[8,4096]{1,0:T(8,128)} async-done(((f32[8,4096]{1,0:T(8,128)}), f32[8,4096]{1,0:T(8,128)}) %all-reduce.12.cloned.1.call-update) | async-done | bytes 131088 | tf_op jit(solution)/shard_map/psum | solution.py:157
  371.3 1.6 copy.29
  (96 shorter events, 25.6 us)
Async XLA Ops:
  8.3 6.8 %collective-permute-start = (f32[10,1,1024]{2,1,0:T(1,128)S(1)}, f32[10,1,1024]{2,1,0:T(1,128)S(1)}, u32[]{:S(2)}, u32[]{:S(2)}) collective-permute-start(f32[10,1,1024]{2,1,0:T(1,128)S(1)} %get-tuple-element.47), channel_id=1, source_target_pairs={{4,0},{8,4},{12,8},{16,12},{20,16},{24,20},{28,24},{5,1},{9,5},{13... | collective-permute-start | bytes 122888 | tf_op jit(solution)/shard_map/ppermute | solution.py:25
  9.6 7.2 %collective-permute-start.1 = (f32[10,1,1024]{2,1,0:T(1,128)S(1)}, f32[10,1,1024]{2,1,0:T(1,128)S(1)}, u32[]{:S(2)}, u32[]{:S(2)}) collective-permute-start(f32[10,1,1024]{2,1,0:T(1,128)S(1)} %get-tuple-element.46), channel_id=1, source_target_pairs={{0,4},{4,8},{8,12},{12,16},{16,20},{20,24},{24,28},{1,5},{5,9},{9,... | collective-permute-start | bytes 122888 | tf_op jit(solution)/shard_map/ppermute | solution.py:23
  15.1 19.6 %copy-start.9 = (f32[10,1,1024]{2,1,0:T(1,128)}, f32[10,1,1024]{2,1,0:T(1,128)S(1)}, u32[]{:S(2)}) copy-start(f32[10,1,1024]{2,1,0:T(1,128)S(1)} %collective-permute-done) | copy-start | bytes 122884
  16.8 18.0 %copy-start.10 = (f32[10,1,1024]{2,1,0:T(1,128)}, f32[10,1,1024]{2,1,0:T(1,128)S(1)}, u32[]{:S(2)}) copy-start(f32[10,1,1024]{2,1,0:T(1,128)S(1)} %collective-permute-done.1) | copy-start | bytes 122884
  18.0 6.5 %collective-permute-start.2 = (f32[10,10,1]{2,1,0:T(8,128)S(1)}, f32[10,10,1]{2,1,0:T(8,128)S(1)}, u32[]{:S(2)}, u32[]{:S(2)}) collective-permute-start(f32[10,10,1]{2,1,0:T(8,128)S(1)} %get-tuple-element.34), channel_id=1, source_target_pairs={{1,0},{2,1},{3,2},{5,4},{6,5},{7,6},{9,8},{10,9},{11,10},{13,12},{... | collective-permute-start | bytes 1208 | tf_op jit(solution)/shard_map/ppermute | solution.py:25
  19.3 5.2 %collective-permute-start.3 = (f32[10,10,1]{2,1,0:T(8,128)S(1)}, f32[10,10,1]{2,1,0:T(8,128)S(1)}, u32[]{:S(2)}, u32[]{:S(2)}) collective-permute-start(f32[10,10,1]{2,1,0:T(8,128)S(1)} %get-tuple-element.35), channel_id=1, source_target_pairs={{0,1},{1,2},{2,3},{4,5},{5,6},{6,7},{8,9},{9,10},{10,11},{12,13},{... | collective-permute-start | bytes 1208 | tf_op jit(solution)/shard_map/ppermute | solution.py:23
  24.5 17.3 %copy-start.7 = (f32[10,10,1]{2,1,0:T(8,128)}, f32[10,10,1]{2,1,0:T(8,128)S(1)}, u32[]{:S(2)}) copy-start(f32[10,10,1]{2,1,0:T(8,128)S(1)} %collective-permute-done.2) | copy-start | bytes 1204
  24.5 17.3 %copy-start.8 = (f32[10,10,1]{2,1,0:T(8,128)}, f32[10,10,1]{2,1,0:T(8,128)S(1)}, u32[]{:S(2)}) copy-start(f32[10,10,1]{2,1,0:T(8,128)S(1)} %collective-permute-done.3) | copy-start | bytes 1204
  26.8 7.9 %collective-permute-start.4 = (f32[10,1,1024]{2,1,0:T(1,128)S(1)}, f32[10,1,1024]{2,1,0:T(1,128)S(1)}, u32[]{:S(2)}, u32[]{:S(2)}) collective-permute-start(f32[10,1,1024]{2,1,0:T(1,128)S(1)} %get-tuple-element.45), channel_id=1, source_target_pairs={{4,0},{8,4},{12,8},{16,12},{20,16},{24,20},{28,24},{5,1},{9,5},{13... | collective-permute-start | bytes 122888 | tf_op jit(solution)/shard_map/ppermute | solution.py:25
  28.1 7.6 %collective-permute-start.5 = (f32[10,1,1024]{2,1,0:T(1,128)S(1)}, f32[10,1,1024]{2,1,0:T(1,128)S(1)}, u32[]{:S(2)}, u32[]{:S(2)}) collective-permute-start(f32[10,1,1024]{2,1,0:T(1,128)S(1)} %get-tuple-element.44), channel_id=1, source_target_pairs={{0,4},{4,8},{8,12},{12,16},{16,20},{20,24},{24,28},{1,5},{5,9},{9,... | collective-permute-start | bytes 122888 | tf_op jit(solution)/shard_map/ppermute | solution.py:23
  34.7 6.6 %copy-start.14 = (s32[32]{0:T(128)}, s32[32]{0:T(128)S(1)}, u32[]{:S(2)}) copy-start(s32[32]{0:T(128)S(1)} %get-tuple-element.51) | copy-start | bytes 388
  34.7 5.5 %copy-start.3 = (f32[10,1,1024]{2,1,0:T(1,128)}, f32[10,1,1024]{2,1,0:T(1,128)S(1)}, u32[]{:S(2)}) copy-start(f32[10,1,1024]{2,1,0:T(1,128)S(1)} %collective-permute-done.4) | copy-start | bytes 122884
  35.6 4.6 %copy-start.5 = (f32[10,1,1024]{2,1,0:T(1,128)}, f32[10,1,1024]{2,1,0:T(1,128)S(1)}, u32[]{:S(2)}) copy-start(f32[10,1,1024]{2,1,0:T(1,128)S(1)} %collective-permute-done.5) | copy-start | bytes 122884
  35.9 5.5 %collective-permute-start.6 = (f32[10,10,1]{2,1,0:T(8,128)S(1)}, f32[10,10,1]{2,1,0:T(8,128)S(1)}, u32[]{:S(2)}, u32[]{:S(2)}) collective-permute-start(f32[10,10,1]{2,1,0:T(8,128)S(1)} %get-tuple-element.33), channel_id=1, source_target_pairs={{1,0},{2,1},{3,2},{5,4},{6,5},{7,6},{9,8},{10,9},{11,10},{13,12},{... | collective-permute-start | bytes 1208 | tf_op jit(solution)/shard_map/ppermute | solution.py:25
  37.2 4.2 %collective-permute-start.7 = (f32[10,10,1]{2,1,0:T(8,128)S(1)}, f32[10,10,1]{2,1,0:T(8,128)S(1)}, u32[]{:S(2)}, u32[]{:S(2)}) collective-permute-start(f32[10,10,1]{2,1,0:T(8,128)S(1)} %get-tuple-element.32), channel_id=1, source_target_pairs={{0,1},{1,2},{2,3},{4,5},{5,6},{6,7},{8,9},{9,10},{10,11},{12,13},{... | collective-permute-start | bytes 1208 | tf_op jit(solution)/shard_map/ppermute | solution.py:23
  41.4 0.6 copy-start.1
  45.4 90.2 %copy-start.2 = (f32[10,10,1]{2,1,0:T(8,128)S(1)}, f32[10,10,1]{2,1,0:T(8,128)}, u32[]{:S(2)}) copy-start(f32[10,10,1]{2,1,0:T(8,128)} %copy-done.1) | copy-start | bytes 1204
  45.4 90.2 %copy-start.4 = (f32[10,1,1024]{2,1,0:T(1,128)S(1)}, f32[10,1,1024]{2,1,0:T(1,128)}, u32[]{:S(2)}) copy-start(f32[10,1,1024]{2,1,0:T(1,128)} %copy-done.3) | copy-start | bytes 122884
  45.4 90.2 %copy-start.6 = (f32[10,1,1024]{2,1,0:T(1,128)S(1)}, f32[10,1,1024]{2,1,0:T(1,128)}, u32[]{:S(2)}) copy-start(f32[10,1,1024]{2,1,0:T(1,128)} %copy-done.5) | copy-start | bytes 122884
  45.5 7.4 %collective-permute-start.8 = (f32[10,1,1024]{2,1,0:T(1,128)S(1)}, f32[10,1,1024]{2,1,0:T(1,128)S(1)}, u32[]{:S(2)}, u32[]{:S(2)}) collective-permute-start(f32[10,1,1024]{2,1,0:T(1,128)S(1)} %get-tuple-element.43), channel_id=1, source_target_pairs={{4,0},{8,4},{12,8},{16,12},{20,16},{24,20},{28,24},{5,1},{9,5},{13... | collective-permute-start | bytes 122888 | tf_op jit(solution)/shard_map/ppermute | solution.py:25
  46.8 7.1 %collective-permute-start.9 = (f32[10,1,1024]{2,1,0:T(1,128)S(1)}, f32[10,1,1024]{2,1,0:T(1,128)S(1)}, u32[]{:S(2)}, u32[]{:S(2)}) collective-permute-start(f32[10,1,1024]{2,1,0:T(1,128)S(1)} %get-tuple-element.42), channel_id=1, source_target_pairs={{0,4},{4,8},{8,12},{12,16},{16,20},{20,24},{24,28},{1,5},{5,9},{9,... | collective-permute-start | bytes 122888 | tf_op jit(solution)/shard_map/ppermute | solution.py:23
  52.9 74.5 %copy-start.13 = (s32[32]{0:T(128)}, s32[32]{0:T(128)S(1)}, u32[]{:S(2)}) copy-start(s32[32]{0:T(128)S(1)} %multiply_add_fusion.2) | copy-start | bytes 388
  54.1 5.5 %collective-permute-start.10 = (f32[10,10,1]{2,1,0:T(8,128)S(1)}, f32[10,10,1]{2,1,0:T(8,128)S(1)}, u32[]{:S(2)}, u32[]{:S(2)}) collective-permute-start(f32[10,10,1]{2,1,0:T(8,128)S(1)} %get-tuple-element.31), channel_id=1, source_target_pairs={{0,1},{1,2},{2,3},{4,5},{5,6},{6,7},{8,9},{9,10},{10,11},{12,13},{... | collective-permute-start | bytes 1208 | tf_op jit(solution)/shard_map/ppermute | solution.py:23
  57.6 5.9 %collective-permute-start.11 = (f32[10,10,1]{2,1,0:T(8,128)S(1)}, f32[10,10,1]{2,1,0:T(8,128)S(1)}, u32[]{:S(2)}, u32[]{:S(2)}) collective-permute-start(f32[10,10,1]{2,1,0:T(8,128)S(1)} %get-tuple-element.30), channel_id=1, source_target_pairs={{1,0},{2,1},{3,2},{5,4},{6,5},{7,6},{9,8},{10,9},{11,10},{13,12},{... | collective-permute-start | bytes 1208 | tf_op jit(solution)/shard_map/ppermute | solution.py:25
  114.6 12.7 %collective-permute-start.12 = (f32[10,1,1024]{2,1,0:T(1,128)S(1)}, f32[10,1,1024]{2,1,0:T(1,128)S(1)}, u32[]{:S(2)}, u32[]{:S(2)}) collective-permute-start(f32[10,1,1024]{2,1,0:T(1,128)S(1)} %get-tuple-element.41), channel_id=1, source_target_pairs={{4,0},{8,4},{12,8},{16,12},{20,16},{24,20},{28,24},{5,1},{9,5},{13... | collective-permute-start | bytes 122888 | tf_op jit(solution)/shard_map/ppermute | solution.py:25
  115.9 11.4 %collective-permute-start.13 = (f32[10,1,1024]{2,1,0:T(1,128)S(1)}, f32[10,1,1024]{2,1,0:T(1,128)S(1)}, u32[]{:S(2)}, u32[]{:S(2)}) collective-permute-start(f32[10,1,1024]{2,1,0:T(1,128)S(1)} %get-tuple-element.40), channel_id=1, source_target_pairs={{0,4},{4,8},{8,12},{12,16},{16,20},{20,24},{24,28},{1,5},{5,9},{9,... | collective-permute-start | bytes 122888 | tf_op jit(solution)/shard_map/ppermute | solution.py:23
  121.4 148.9 %all-to-all-start = ((s32[8,1,8]{2,1,0:T(1,128)}), s32[8,1,8]{2,1,0:T(1,128)}, u32[]{:S(2)}, u32[]{:S(2)}) async-start(s32[8,1,8]{2,1,0:T(1,128)} %bitcast), calls=%async_computation | async-start | bytes 8192 | tf_op jit(solution)/shard_map/all_to_all | solution.py:146
  127.6 3.8 collective-permute-start.14
  128.9 5.5 %collective-permute-start.15 = (f32[10,10,1]{2,1,0:T(8,128)S(1)}, f32[10,10,1]{2,1,0:T(8,128)S(1)}, u32[]{:S(2)}, u32[]{:S(2)}) collective-permute-start(f32[10,10,1]{2,1,0:T(8,128)S(1)} %get-tuple-element.28), channel_id=1, source_target_pairs={{1,0},{2,1},{3,2},{5,4},{6,5},{7,6},{9,8},{10,9},{11,10},{13,12},{... | collective-permute-start | bytes 1208 | tf_op jit(solution)/shard_map/ppermute | solution.py:25
  186.2 8.2 %collective-permute-start.16 = (f32[10,1,1024]{2,1,0:T(1,128)S(1)}, f32[10,1,1024]{2,1,0:T(1,128)S(1)}, u32[]{:S(2)}, u32[]{:S(2)}) collective-permute-start(f32[10,1,1024]{2,1,0:T(1,128)S(1)} %get-tuple-element.39), channel_id=1, source_target_pairs={{4,0},{8,4},{12,8},{16,12},{20,16},{24,20},{28,24},{5,1},{9,5},{13... | collective-permute-start | bytes 122888 | tf_op jit(solution)/shard_map/ppermute | solution.py:25
  187.5 6.9 %collective-permute-start.17 = (f32[10,1,1024]{2,1,0:T(1,128)S(1)}, f32[10,1,1024]{2,1,0:T(1,128)S(1)}, u32[]{:S(2)}, u32[]{:S(2)}) collective-permute-start(f32[10,1,1024]{2,1,0:T(1,128)S(1)} %get-tuple-element.38), channel_id=1, source_target_pairs={{0,4},{4,8},{8,12},{12,16},{16,20},{20,24},{24,28},{1,5},{5,9},{9,... | collective-permute-start | bytes 122888 | tf_op jit(solution)/shard_map/ppermute | solution.py:23
  196.5 8.0 %collective-permute-start.18 = (f32[10,10,1]{2,1,0:T(8,128)S(1)}, f32[10,10,1]{2,1,0:T(8,128)S(1)}, u32[]{:S(2)}, u32[]{:S(2)}) collective-permute-start(f32[10,10,1]{2,1,0:T(8,128)S(1)} %get-tuple-element.27), channel_id=1, source_target_pairs={{0,1},{1,2},{2,3},{4,5},{5,6},{6,7},{8,9},{9,10},{10,11},{12,13},{... | collective-permute-start | bytes 1208 | tf_op jit(solution)/shard_map/ppermute | solution.py:23
  197.8 6.7 %collective-permute-start.19 = (f32[10,10,1]{2,1,0:T(8,128)S(1)}, f32[10,10,1]{2,1,0:T(8,128)S(1)}, u32[]{:S(2)}, u32[]{:S(2)}) collective-permute-start(f32[10,10,1]{2,1,0:T(8,128)S(1)} %get-tuple-element.26), channel_id=1, source_target_pairs={{1,0},{2,1},{3,2},{5,4},{6,5},{7,6},{9,8},{10,9},{11,10},{13,12},{... | collective-permute-start | bytes 1208 | tf_op jit(solution)/shard_map/ppermute | solution.py:25
  204.5 134.8 %copy-start = (f32[10,8,1024]{2,1,0:T(8,128)S(1)}, f32[10,8,1024]{2,1,0:T(8,128)}, u32[]{:S(2)}) copy-start(f32[10,8,1024]{2,1,0:T(8,128)} %param.21) | copy-start | bytes 983044
  260.9 8.1 %collective-permute-start.20 = (f32[10,1,1024]{2,1,0:T(1,128)S(1)}, f32[10,1,1024]{2,1,0:T(1,128)S(1)}, u32[]{:S(2)}, u32[]{:S(2)}) collective-permute-start(f32[10,1,1024]{2,1,0:T(1,128)S(1)} %get-tuple-element.37), channel_id=1, source_target_pairs={{4,0},{8,4},{12,8},{16,12},{20,16},{24,20},{28,24},{5,1},{9,5},{13... | collective-permute-start | bytes 122888 | tf_op jit(solution)/shard_map/ppermute | solution.py:25
  262.2 6.8 %collective-permute-start.21 = (f32[10,1,1024]{2,1,0:T(1,128)S(1)}, f32[10,1,1024]{2,1,0:T(1,128)S(1)}, u32[]{:S(2)}, u32[]{:S(2)}) collective-permute-start(f32[10,1,1024]{2,1,0:T(1,128)S(1)} %get-tuple-element.36), channel_id=1, source_target_pairs={{0,4},{4,8},{8,12},{12,16},{16,20},{20,24},{24,28},{1,5},{5,9},{9,... | collective-permute-start | bytes 122888 | tf_op jit(solution)/shard_map/ppermute | solution.py:23
  269.0 0.6 copy-start.11
  269.6 0.6 copy-start.12
  270.3 67.1 %all-to-all-start.1 = ((f32[8,8,1024]{2,1,0:T(8,128)}), f32[8,8,1024]{2,1,0:T(8,128)}, u32[]{:S(2)}, u32[]{:S(2)}) async-start(f32[8,8,1024]{2,1,0:T(8,128)} %convolution_bitcast_fusion), calls=%async_computation.1 | async-start | bytes 524288 | tf_op jit(solution)/shard_map/all_to_all | solution.py:145
  276.6 94.7 %all-reduce.12.cloned.1.call-start = ((), (), s32[]{:S(2)}) async-start(), calls=%async_computation.2 | async-start | bytes 262144 | tf_op jit(solution)/shard_map/psum | solution.py:157
  277.4 6.9 %collective-permute-start.22 = (f32[10,10,1]{2,1,0:T(8,128)}, f32[10,10,1]{2,1,0:T(8,128)}, u32[]{:S(2)}, u32[]{:S(2)}) collective-permute-start(f32[10,10,1]{2,1,0:T(8,128)} %get-tuple-element.25), channel_id=1, source_target_pairs={{0,1},{1,2},{2,3},{4,5},{5,6},{6,7},{8,9},{9,10},{10,11},{12,13},{... | collective-permute-start | bytes 1208 | tf_op jit(solution)/shard_map/ppermute | solution.py:23
  279.3 5.4 %collective-permute-start.23 = (f32[10,10,1]{2,1,0:T(8,128)}, f32[10,10,1]{2,1,0:T(8,128)}, u32[]{:S(2)}, u32[]{:S(2)}) collective-permute-start(f32[10,10,1]{2,1,0:T(8,128)} %get-tuple-element.24), channel_id=1, source_target_pairs={{1,0},{2,1},{3,2},{5,4},{6,5},{7,6},{9,8},{10,9},{11,10},{13,12},{... | collective-permute-start | bytes 1208 | tf_op jit(solution)/shard_map/ppermute | solution.py:25
Sparse Core Ops, SparseCore 0:
  339.4 31.8 all-reduce.11
where the time goes:
time: 382 us; the launch traced here: 380 us
  blocking collectives  176 us (46%)
  starting transfers between devices  72.7 us (19%)
  waiting for transfers between devices  42 us (11%)
  other arithmetic  34 us (9%)
  between operations  27.8 us (7%)
  local copies, waits for them, and re-layouts  18.5 us (5%)
  matrix products  8.41 us (2%)
    psum x4, blocking collectives, paired_totals(): lax.psum((jnp.sum(residual * residual), jnp.sum(residual * image)), ('til...  176 us
    ppermute x12, starting transfers between devices, extended(): lax.ppermute(tail, axis, [(i, (i + 1) % count) for i in range(ends)])  44.9 us
    psum x1, waiting for transfers between devices, body(): totals = lax.psum(partial_sums, 'lev')  31.1 us
    ppermute x12, starting transfers between devices, extended(): lax.ppermute(head, axis, [((i + 1) % count, i) for i in range(ends)])  15.7 us
    reduce_sum x4, other arithmetic, paired_totals(): jnp.sum(residual * image)  14 us
  transfers between devices with their start and end apart: 27, of which 7 were waited for; matrix products, arithmetic and copies ran while one was open for 11% of the time, Pallas kernels for 0%

commit v1 on v0

--- a/solution.py
+++ b/solution.py
@@ -10,6 +10,11 @@
 VISC_FLOOR = 0.25
 VERTICAL = 4.0
 SMB_WEIGHT = 0.5
+
+
+def one_after_other(value, axis_one, axis_two):
+    partial = lax.psum(value, axis_one)
+    return lax.psum(partial, axis_two)
 
 
 def extended(cells, sides, width):
@@ -71,7 +76,9 @@
 
 
 def paired_totals(residual, image):
-    return lax.psum((jnp.sum(residual * residual), jnp.sum(residual * image)), ("tiles", "lev"))
+    return one_after_other(
+        (jnp.sum(residual * residual), jnp.sum(residual * image)), "lev", "tiles"
+    )
 
 
 def krylov_merged(faces, rhs, start):

time: 382 us -> 324 us (0.85)
  blocking collectives: 176 us -> 127 us
  starting transfers between devices: 72.7 us -> 67.7 us
    psum x4 -> x8, blocking collectives: 176 us -> 127 us  [the longest x4 89.8 us: one_after_other(): return lax.psum(partial, axis_two)]
  transfers between devices with their start and end apart: 27 -> 27, of which waited for: 7 -> 6; matrix products, arithmetic and copies ran while one was open for 11% -> 13% of each run, Pallas kernels for 0% -> 0%
where the time goes in v1:
time: 324 us; the launch traced here: 322 us
  blocking collectives  127 us (39%)
  starting transfers between devices  67.7 us (21%)
  waiting for transfers between devices  38.3 us (12%)
  other arithmetic  34 us (10%)
  between operations  28 us (9%)
  local copies, waits for them, and re-layouts  18.4 us (6%)
  matrix products  8.41 us (3%)
    psum x4, blocking collectives, one_after_other(): return lax.psum(partial, axis_two)  89.8 us
    ppermute x12, starting transfers between devices, extended(): lax.ppermute(tail, axis, [(i, (i + 1) % count) for i in range(ends)])  44.1 us
    psum x4, blocking collectives, one_after_other(): partial = lax.psum(value, axis_one)  37.4 us
    psum x1, waiting for transfers between devices, body(): totals = lax.psum(partial_sums, 'lev')  28.3 us
    ppermute x12, starting transfers between devices, extended(): lax.ppermute(head, axis, [((i + 1) % count, i) for i in range(ends)])  15.7 us
    reduce_sum x4, other arithmetic, paired_totals(): jnp.sum(residual * image)  13.9 us
    concatenate x6, local copies, waits for them, and re-layouts, extended(): jnp.concatenate([lax.ppermute(tail, axis, [(i, (i + 1) % count) for i in...  7.39 us
  transfers between devices with their start and end apart: 27, of which 6 were waited for; matrix products, arithmetic and copies ran while one was open for 13% of the time, Pallas kernels for 0%

profile of v1, /device:TPU:0, one launch (start us, length us, event | category | flops | bytes accessed | tf_op | source)
XLA Modules:
  0.0 322.0 jit_solution(923926127803403673)
XLA Ops:
  8.3 1.3 collective-permute-start
  9.6 5.5 %collective-permute-start.1 = (f32[10,1,1024]{2,1,0:T(1,128)S(1)}, f32[10,1,1024]{2,1,0:T(1,128)S(1)}, u32[]{:S(2)}, u32[]{:S(2)}) collective-permute-start(f32[10,1,1024]{2,1,0:T(1,128)S(1)} %get-tuple-element.54), channel_id=1, source_target_pairs={{0,4},{4,8},{8,12},{12,16},{16,20},{20,24},{24,28},{1,5},{5,9},{9,... | collective-permute-start | bytes 122888 | tf_op jit(solution)/shard_map/ppermute | solution.py:28
  15.2 1.6 collective-permute-done.1
  18.0 1.3 collective-permute-start.2
  19.3 3.0 collective-permute-start.3
  22.3 1.4 add_multiply_fusion
  24.5 2.2 power_multiply_fusion
  26.8 1.3 collective-permute-start.4
  28.1 5.4 %collective-permute-start.5 = (f32[10,1,1024]{2,1,0:T(1,128)S(1)}, f32[10,1,1024]{2,1,0:T(1,128)S(1)}, u32[]{:S(2)}, u32[]{:S(2)}) collective-permute-start(f32[10,1,1024]{2,1,0:T(1,128)S(1)} %get-tuple-element.52), channel_id=1, source_target_pairs={{0,4},{4,8},{8,12},{12,16},{16,20},{20,24},{24,28},{1,5},{5,9},{9,... | collective-permute-start | bytes 122888 | tf_op jit(solution)/shard_map/ppermute | solution.py:28
  35.9 1.3 collective-permute-start.6
  37.2 3.0 collective-permute-start.7
  42.0 3.4 %fusion.11 = (f32[10,8,1024]{2,1,0:T(8,128)S(1)}, f32[10,8,1024]{2,1,0:T(8,128)S(1)}, f32[10,8,1024]{2,1,0:T(8,128)S(1)}) fusion(f32[10,10,1026]{2,1,0:T(8,128)S(1)} %concatenate.125, f32[10,8,1024]{2,1,0:T(8,128)} %param.21, f32[10,8,1024]{2,1,0:T(8,128)} %param.20, f32[10,1,1024]{2,1,0:T(1,128)} %copy-done.9, f32[10,1,1024]{2,1,0:T(1,128)} %copy-done.10, ...), kind=kLoop, calls=%fused_computation.32 | loop fusion | flops 3686400 | bytes 3017856 | tf_op jit(solution)/shard_map/sub | solution.py:86
  45.5 1.3 collective-permute-start.8
  46.8 5.4 %collective-permute-start.9 = (f32[10,1,1024]{2,1,0:T(1,128)S(1)}, f32[10,1,1024]{2,1,0:T(1,128)S(1)}, u32[]{:S(2)}, u32[]{:S(2)}) collective-permute-start(f32[10,1,1024]{2,1,0:T(1,128)S(1)} %get-tuple-element.50), channel_id=1, source_target_pairs={{0,4},{4,8},{8,12},{12,16},{16,20},{20,24},{24,28},{1,5},{5,9},{9,... | collective-permute-start | bytes 122888 | tf_op jit(solution)/shard_map/ppermute | solution.py:28
  54.1 3.5 %collective-permute-start.10 = (f32[10,10,1]{2,1,0:T(8,128)S(1)}, f32[10,10,1]{2,1,0:T(8,128)S(1)}, u32[]{:S(2)}, u32[]{:S(2)}) collective-permute-start(f32[10,10,1]{2,1,0:T(8,128)S(1)} %get-tuple-element.39), channel_id=1, source_target_pairs={{0,1},{1,2},{2,3},{4,5},{5,6},{6,7},{8,9},{9,10},{10,11},{12,13},{... | collective-permute-start | bytes 1208 | tf_op jit(solution)/shard_map/ppermute | solution.py:28
  57.6 1.3 collective-permute-start.11
  59.7 3.8 %collective-permute-done.11 = f32[10,10,1]{2,1,0:T(8,128)S(1)} collective-permute-done((f32[10,10,1]{2,1,0:T(8,128)S(1)}, f32[10,10,1]{2,1,0:T(8,128)S(1)}, u32[]{:S(2)}, u32[]{:S(2)}) %collective-permute-start.11) | collective-permute-done | bytes 432 | tf_op jit(solution)/shard_map/ppermute | solution.py:30
  64.6 3.3 %multiply_reduce_fusion.5 = (f32[]{:T(128)}, f32[]{:T(128)}, f32[10,8,1024]{2,1,0:T(8,128)S(1)}) fusion(f32[10,8,1024]{2,1,0:T(8,128)S(1)} %get-tuple-element.29, f32[10,1,1024]{2,1,0:T(1,128)S(1)} %collective-permute-done.8, f32[10,1,1024]{2,1,0:T(1,128)S(1)} %collective-permute-done.9, f32[10,10,1]{2,1,0:T(8,128)S(1)} %collective-permute-done.10, ...), kind=kLoop, calls=%fused_computation.149 | loop fusion | flops 3522558 | bytes 2247016 | tf_op jit(solution)/shard_map/reduce_sum | solution.py:80
  68.0 9.3 %all-reduce.13 = (f32[]{:T(128)}, f32[]{:T(128)}) all-reduce(f32[]{:T(128)} %get-tuple-element.7, f32[]{:T(128)} %get-tuple-element.6), channel_id=1, replica_groups=mesh['tiles'=8,'lev'=4] {'lev'}, use_global_device_ids=true, to_apply=%region_4.5 | all-reduce | flops 2 | bytes 16 | tf_op jit(solution)/shard_map/psum | solution.py:16
  77.3 25.4 %all-reduce.9 = (f32[]{:T(128)}, f32[]{:T(128)}) all-reduce(f32[]{:T(128)} %get-tuple-element.22, f32[]{:T(128)} %get-tuple-element.23), channel_id=1, replica_groups=mesh['tiles'=8,'lev'=4] {'tiles'}, use_global_device_ids=true, to_apply=%region_5.6 | all-reduce | flops 2 | bytes 16 | tf_op jit(solution)/shard_map/psum | solution.py:17
  104.1 1.3 collective-permute-start.12
  105.4 4.5 %collective-permute-start.13 = (f32[10,1,1024]{2,1,0:T(1,128)S(1)}, f32[10,1,1024]{2,1,0:T(1,128)S(1)}, u32[]{:S(2)}, u32[]{:S(2)}) collective-permute-start(f32[10,1,1024]{2,1,0:T(1,128)S(1)} %get-tuple-element.48), channel_id=1, source_target_pairs={{0,4},{4,8},{8,12},{12,16},{16,20},{20,24},{24,28},{1,5},{5,9},{9,... | collective-permute-start | bytes 122888 | tf_op jit(solution)/shard_map/ppermute | solution.py:28
  110.6 3.8 %all-to-all-start = ((s32[8,1,8]{2,1,0:T(1,128)}), s32[8,1,8]{2,1,0:T(1,128)}, u32[]{:S(2)}, u32[]{:S(2)}) async-start(s32[8,1,8]{2,1,0:T(1,128)} %bitcast), calls=%async_computation | async-start | bytes 8192 | tf_op jit(solution)/shard_map/all_to_all | solution.py:153
  114.7 1.3 collective-permute-start.14
  118.5 2.5 collective-permute-done.15
  122.2 3.3 %multiply_reduce_fusion.3 = (f32[]{:T(128)}, f32[]{:T(128)}, f32[10,8,1024]{2,1,0:T(8,128)S(1)}) fusion(f32[10,8,1024]{2,1,0:T(8,128)S(1)} %multiply_subtract_fusion.2, f32[10,1,1024]{2,1,0:T(1,128)S(1)} %collective-permute-done.12, f32[10,1,1024]{2,1,0:T(1,128)S(1)} %collective-permute-done.13, f32[10,10,1]{2,1,0:T(8,128)S(1)} %collective-permute-done.14, ...), kind=kLoop, calls=%fused_computation.146 | loop fusion | flops 3522558 | bytes 2247016 | tf_op jit(solution)/shard_map/reduce_sum | solution.py:80
  125.5 9.4 %all-reduce.12 = (f32[]{:T(128)}, f32[]{:T(128)}) all-reduce(f32[]{:T(128)} %get-tuple-element.5, f32[]{:T(128)} %get-tuple-element.4), channel_id=1, replica_groups=mesh['tiles'=8,'lev'=4] {'lev'}, use_global_device_ids=true, to_apply=%region_10.11 | all-reduce | flops 2 | bytes 16 | tf_op jit(solution)/shard_map/psum | solution.py:16
  134.9 22.4 %all-reduce.8 = (f32[]{:T(128)}, f32[]{:T(128)}) all-reduce(f32[]{:T(128)} %get-tuple-element.20, f32[]{:T(128)} %get-tuple-element.21), channel_id=1, replica_groups=mesh['tiles'=8,'lev'=4] {'tiles'}, use_global_device_ids=true, to_apply=%region_11.12 | all-reduce | flops 2 | bytes 16 | tf_op jit(solution)/shard_map/psum | solution.py:17
  163.2 4.5 %collective-permute-start.17 = (f32[10,1,1024]{2,1,0:T(1,128)S(1)}, f32[10,1,1024]{2,1,0:T(1,128)S(1)}, u32[]{:S(2)}, u32[]{:S(2)}) collective-permute-start(f32[10,1,1024]{2,1,0:T(1,128)S(1)} %get-tuple-element.46), channel_id=1, source_target_pairs={{0,4},{4,8},{8,12},{12,16},{16,20},{20,24},{24,28},{1,5},{5,9},{9,... | collective-permute-start | bytes 122888 | tf_op jit(solution)/shard_map/ppermute | solution.py:28
  171.8 1.3 collective-permute-start.18
  173.1 1.5 collective-permute-start.19
  174.6 5.2 %fusion.74 = f32[32,1,1024]{2,1,0:T(1,128)} fusion(bf16[32,128,1024]{2,1,0:T(8,128)(2,1)} %param.12, bf16[32,128,1]{1,0,2:T(8,128)(2,1)S(1)} %bitcast.19), kind=kOutput, calls=%fused_computation.159 | convolution fusion | flops 8388608 | bytes 8527872 | tf_op jit(solution)/shard_map/bl,blt->bt/dot_general | solution.py:131
  179.8 2.3 concatenate.141
  182.1 3.9 %multiply_reduce_fusion.1 = (f32[]{:T(128)}, f32[]{:T(128)}, f32[10,8,1024]{2,1,0:T(8,128)}) fusion(f32[10,8,1024]{2,1,0:T(8,128)S(1)} %multiply_subtract_fusion.1, f32[10,1,1024]{2,1,0:T(1,128)S(1)} %collective-permute-done.16, f32[10,1,1024]{2,1,0:T(1,128)S(1)} %collective-permute-done.17, f32[10,10,1]{2,1,0:T(8,128)S(1)} %collective-permute-done.18, ...), kind=kLoop, calls=%fused_computation.142 | loop fusion | flops 3522558 | bytes 2247016 | tf_op jit(solution)/shard_map/reduce_sum | solution.py:80
  186.0 9.3 %all-reduce.11 = (f32[]{:T(128)}, f32[]{:T(128)}) all-reduce(f32[]{:T(128)} %get-tuple-element.3, f32[]{:T(128)} %get-tuple-element.2), channel_id=1, replica_groups=mesh['tiles'=8,'lev'=4] {'lev'}, use_global_device_ids=true, to_apply=%region_16.17 | all-reduce | flops 2 | bytes 16 | tf_op jit(solution)/shard_map/psum | solution.py:16
  195.3 19.7 %all-reduce.7 = (f32[]{:T(128)}, f32[]{:T(128)}) all-reduce(f32[]{:T(128)} %get-tuple-element.18, f32[]{:T(128)} %get-tuple-element.19), channel_id=1, replica_groups=mesh['tiles'=8,'lev'=4] {'tiles'}, use_global_device_ids=true, to_apply=%region_17.18 | all-reduce | flops 2 | bytes 16 | tf_op jit(solution)/shard_map/psum | solution.py:17
  218.7 1.7 multiply_reduce_fusion
  221.8 4.5 %collective-permute-start.21 = (f32[10,1,1024]{2,1,0:T(1,128)S(1)}, f32[10,1,1024]{2,1,0:T(1,128)S(1)}, u32[]{:S(2)}, u32[]{:S(2)}) collective-permute-start(f32[10,1,1024]{2,1,0:T(1,128)S(1)} %get-tuple-element.44), channel_id=1, source_target_pairs={{0,4},{4,8},{8,12},{12,16},{16,20},{20,24},{24,28},{1,5},{5,9},{9,... | collective-permute-start | bytes 122888 | tf_op jit(solution)/shard_map/ppermute | solution.py:28
  226.4 2.0 convolution_bitcast_fusion
  229.7 4.1 %all-to-all-start.1 = ((f32[8,8,1024]{2,1,0:T(8,128)}), f32[8,8,1024]{2,1,0:T(8,128)}, u32[]{:S(2)}, u32[]{:S(2)}) async-start(f32[8,8,1024]{2,1,0:T(8,128)} %convolution_bitcast_fusion), calls=%async_computation.1 | async-start | bytes 524288 | tf_op jit(solution)/shard_map/all_to_all | solution.py:152
  234.5 1.9 collective-permute-start.22
  238.3 1.8 reduce.3
  241.4 2.1 concatenate.147
  243.5 3.3 %fusion.70 = f32[]{:T(128)} fusion(f32[10,8,1024]{2,1,0:T(8,128)S(1)} %get-tuple-element.25, f32[10,1,1024]{2,1,0:T(1,128)} %copy-done.11, f32[10,1,1024]{2,1,0:T(1,128)} %copy-done.12, f32[10,10,1]{2,1,0:T(8,128)} %collective-permute-done.22, f32[10,10,1]{2,1,0:T(8,128)} %collective-permute-done.23, f32[10,8,1024]{2,1,0:T(8,128)S(1)} %get-tuple-element.30, ...), kind=kLoop, calls=%fused_computation.153 | loop fusion | flops 3358719 | bytes 1919332 | tf_op jit(solution)/shard_map/reduce_sum | solution.py:80
  246.8 9.4 %all-reduce.10 = (f32[]{:T(128)}, f32[]{:T(128)}) all-reduce(f32[]{:T(128)} %get-tuple-element.24, f32[]{:T(128)} %fusion.70), channel_id=1, replica_groups=mesh['tiles'=8,'lev'=4] {'lev'}, use_global_device_ids=true, to_apply=%region_22.23 | all-reduce | flops 2 | bytes 16 | tf_op jit(solution)/shard_map/psum | solution.py:16
  256.2 22.3 %all-reduce.6 = (f32[]{:T(128)}, f32[]{:T(128)}) all-reduce(f32[]{:T(128)} %get-tuple-element.16, f32[]{:T(128)} %get-tuple-element.17), channel_id=1, replica_groups=mesh['tiles'=8,'lev'=4] {'tiles'}, use_global_device_ids=true, to_apply=%region_23.24 | all-reduce | flops 2 | bytes 16 | tf_op jit(solution)/shard_map/psum | solution.py:17
  285.2 28.3 %all-reduce.16.cloned.1.call-done = f32[8,4096]{1,0:T(8,128)} async-done(((f32[8,4096]{1,0:T(8,128)}), f32[8,4096]{1,0:T(8,128)}) %all-reduce.16.cloned.1.call-update) | async-done | bytes 131088 | tf_op jit(solution)/shard_map/psum | solution.py:164
  313.5 1.6 copy.29
  (100 shorter events, 30.4 us)
Async XLA Ops:
  8.3 6.8 %collective-permute-start = (f32[10,1,1024]{2,1,0:T(1,128)S(1)}, f32[10,1,1024]{2,1,0:T(1,128)S(1)}, u32[]{:S(2)}, u32[]{:S(2)}) collective-permute-start(f32[10,1,1024]{2,1,0:T(1,128)S(1)} %get-tuple-element.55), channel_id=1, source_target_pairs={{4,0},{8,4},{12,8},{16,12},{20,16},{24,20},{28,24},{5,1},{9,5},{13... | collective-permute-start | bytes 122888 | tf_op jit(solution)/shard_map/ppermute | solution.py:30
  9.6 7.2 %collective-permute-start.1 = (f32[10,1,1024]{2,1,0:T(1,128)S(1)}, f32[10,1,1024]{2,1,0:T(1,128)S(1)}, u32[]{:S(2)}, u32[]{:S(2)}) collective-permute-start(f32[10,1,1024]{2,1,0:T(1,128)S(1)} %get-tuple-element.54), channel_id=1, source_target_pairs={{0,4},{4,8},{8,12},{12,16},{16,20},{20,24},{24,28},{1,5},{5,9},{9,... | collective-permute-start | bytes 122888 | tf_op jit(solution)/shard_map/ppermute | solution.py:28
  15.1 19.7 %copy-start.9 = (f32[10,1,1024]{2,1,0:T(1,128)}, f32[10,1,1024]{2,1,0:T(1,128)S(1)}, u32[]{:S(2)}) copy-start(f32[10,1,1024]{2,1,0:T(1,128)S(1)} %collective-permute-done) | copy-start | bytes 122884
  16.8 18.0 %copy-start.10 = (f32[10,1,1024]{2,1,0:T(1,128)}, f32[10,1,1024]{2,1,0:T(1,128)S(1)}, u32[]{:S(2)}) copy-start(f32[10,1,1024]{2,1,0:T(1,128)S(1)} %collective-permute-done.1) | copy-start | bytes 122884
  18.0 6.5 %collective-permute-start.2 = (f32[10,10,1]{2,1,0:T(8,128)S(1)}, f32[10,10,1]{2,1,0:T(8,128)S(1)}, u32[]{:S(2)}, u32[]{:S(2)}) collective-permute-start(f32[10,10,1]{2,1,0:T(8,128)S(1)} %get-tuple-element.42), channel_id=1, source_target_pairs={{1,0},{2,1},{3,2},{5,4},{6,5},{7,6},{9,8},{10,9},{11,10},{13,12},{... | collective-permute-start | bytes 1208 | tf_op jit(solution)/shard_map/ppermute | solution.py:30
  19.3 5.2 %collective-permute-start.3 = (f32[10,10,1]{2,1,0:T(8,128)S(1)}, f32[10,10,1]{2,1,0:T(8,128)S(1)}, u32[]{:S(2)}, u32[]{:S(2)}) collective-permute-start(f32[10,10,1]{2,1,0:T(8,128)S(1)} %get-tuple-element.43), channel_id=1, source_target_pairs={{0,1},{1,2},{2,3},{4,5},{5,6},{6,7},{8,9},{9,10},{10,11},{12,13},{... | collective-permute-start | bytes 1208 | tf_op jit(solution)/shard_map/ppermute | solution.py:28
  24.5 17.3 %copy-start.7 = (f32[10,10,1]{2,1,0:T(8,128)}, f32[10,10,1]{2,1,0:T(8,128)S(1)}, u32[]{:S(2)}) copy-start(f32[10,10,1]{2,1,0:T(8,128)S(1)} %collective-permute-done.2) | copy-start | bytes 1204
  24.5 17.3 %copy-start.8 = (f32[10,10,1]{2,1,0:T(8,128)}, f32[10,10,1]{2,1,0:T(8,128)S(1)}, u32[]{:S(2)}) copy-start(f32[10,10,1]{2,1,0:T(8,128)S(1)} %collective-permute-done.3) | copy-start | bytes 1204
  26.8 8.0 %collective-permute-start.4 = (f32[10,1,1024]{2,1,0:T(1,128)S(1)}, f32[10,1,1024]{2,1,0:T(1,128)S(1)}, u32[]{:S(2)}, u32[]{:S(2)}) collective-permute-start(f32[10,1,1024]{2,1,0:T(1,128)S(1)} %get-tuple-element.53), channel_id=1, source_target_pairs={{4,0},{8,4},{12,8},{16,12},{20,16},{24,20},{28,24},{5,1},{9,5},{13... | collective-permute-start | bytes 122888 | tf_op jit(solution)/shard_map/ppermute | solution.py:30
  28.1 7.6 %collective-permute-start.5 = (f32[10,1,1024]{2,1,0:T(1,128)S(1)}, f32[10,1,1024]{2,1,0:T(1,128)S(1)}, u32[]{:S(2)}, u32[]{:S(2)}) collective-permute-start(f32[10,1,1024]{2,1,0:T(1,128)S(1)} %get-tuple-element.52), channel_id=1, source_target_pairs={{0,4},{4,8},{8,12},{12,16},{16,20},{20,24},{24,28},{1,5},{5,9},{9,... | collective-permute-start | bytes 122888 | tf_op jit(solution)/shard_map/ppermute | solution.py:28
  34.8 6.6 %copy-start.14 = (s32[32]{0:T(128)}, s32[32]{0:T(128)S(1)}, u32[]{:S(2)}) copy-start(s32[32]{0:T(128)S(1)} %get-tuple-element.59) | copy-start | bytes 388
  34.8 5.4 %copy-start.3 = (f32[10,1,1024]{2,1,0:T(1,128)}, f32[10,1,1024]{2,1,0:T(1,128)S(1)}, u32[]{:S(2)}) copy-start(f32[10,1,1024]{2,1,0:T(1,128)S(1)} %collective-permute-done.4) | copy-start | bytes 122884
  35.7 4.6 %copy-start.5 = (f32[10,1,1024]{2,1,0:T(1,128)}, f32[10,1,1024]{2,1,0:T(1,128)S(1)}, u32[]{:S(2)}) copy-start(f32[10,1,1024]{2,1,0:T(1,128)S(1)} %collective-permute-done.5) | copy-start | bytes 122884
  35.9 5.5 %collective-permute-start.6 = (f32[10,10,1]{2,1,0:T(8,128)S(1)}, f32[10,10,1]{2,1,0:T(8,128)S(1)}, u32[]{:S(2)}, u32[]{:S(2)}) collective-permute-start(f32[10,10,1]{2,1,0:T(8,128)S(1)} %get-tuple-element.41), channel_id=1, source_target_pairs={{1,0},{2,1},{3,2},{5,4},{6,5},{7,6},{9,8},{10,9},{11,10},{13,12},{... | collective-permute-start | bytes 1208 | tf_op jit(solution)/shard_map/ppermute | solution.py:30
  37.2 4.2 %collective-permute-start.7 = (f32[10,10,1]{2,1,0:T(8,128)S(1)}, f32[10,10,1]{2,1,0:T(8,128)S(1)}, u32[]{:S(2)}, u32[]{:S(2)}) collective-permute-start(f32[10,10,1]{2,1,0:T(8,128)S(1)} %get-tuple-element.40), channel_id=1, source_target_pairs={{0,1},{1,2},{2,3},{4,5},{5,6},{6,7},{8,9},{9,10},{10,11},{12,13},{... | collective-permute-start | bytes 1208 | tf_op jit(solution)/shard_map/ppermute | solution.py:28
  41.4 0.7 copy-start.1
  45.4 76.8 %copy-start.2 = (f32[10,10,1]{2,1,0:T(8,128)S(1)}, f32[10,10,1]{2,1,0:T(8,128)}, u32[]{:S(2)}) copy-start(f32[10,10,1]{2,1,0:T(8,128)} %copy-done.1) | copy-start | bytes 1204
  45.4 76.7 %copy-start.4 = (f32[10,1,1024]{2,1,0:T(1,128)S(1)}, f32[10,1,1024]{2,1,0:T(1,128)}, u32[]{:S(2)}) copy-start(f32[10,1,1024]{2,1,0:T(1,128)} %copy-done.3) | copy-start | bytes 122884
  45.4 76.7 %copy-start.6 = (f32[10,1,1024]{2,1,0:T(1,128)S(1)}, f32[10,1,1024]{2,1,0:T(1,128)}, u32[]{:S(2)}) copy-start(f32[10,1,1024]{2,1,0:T(1,128)} %copy-done.5) | copy-start | bytes 122884
  45.5 7.4 %collective-permute-start.8 = (f32[10,1,1024]{2,1,0:T(1,128)S(1)}, f32[10,1,1024]{2,1,0:T(1,128)S(1)}, u32[]{:S(2)}, u32[]{:S(2)}) collective-permute-start(f32[10,1,1024]{2,1,0:T(1,128)S(1)} %get-tuple-element.51), channel_id=1, source_target_pairs={{4,0},{8,4},{12,8},{16,12},{20,16},{24,20},{28,24},{5,1},{9,5},{13... | collective-permute-start | bytes 122888 | tf_op jit(solution)/shard_map/ppermute | solution.py:30
  46.8 7.1 %collective-permute-start.9 = (f32[10,1,1024]{2,1,0:T(1,128)S(1)}, f32[10,1,1024]{2,1,0:T(1,128)S(1)}, u32[]{:S(2)}, u32[]{:S(2)}) collective-permute-start(f32[10,1,1024]{2,1,0:T(1,128)S(1)} %get-tuple-element.50), channel_id=1, source_target_pairs={{0,4},{4,8},{8,12},{12,16},{16,20},{20,24},{24,28},{1,5},{5,9},{9,... | collective-permute-start | bytes 122888 | tf_op jit(solution)/shard_map/ppermute | solution.py:28
  52.9 61.6 %copy-start.13 = (s32[32]{0:T(128)}, s32[32]{0:T(128)S(1)}, u32[]{:S(2)}) copy-start(s32[32]{0:T(128)S(1)} %multiply_add_fusion.2) | copy-start | bytes 388
  54.1 5.5 %collective-permute-start.10 = (f32[10,10,1]{2,1,0:T(8,128)S(1)}, f32[10,10,1]{2,1,0:T(8,128)S(1)}, u32[]{:S(2)}, u32[]{:S(2)}) collective-permute-start(f32[10,10,1]{2,1,0:T(8,128)S(1)} %get-tuple-element.39), channel_id=1, source_target_pairs={{0,1},{1,2},{2,3},{4,5},{5,6},{6,7},{8,9},{9,10},{10,11},{12,13},{... | collective-permute-start | bytes 1208 | tf_op jit(solution)/shard_map/ppermute | solution.py:28
  57.6 5.9 %collective-permute-start.11 = (f32[10,10,1]{2,1,0:T(8,128)S(1)}, f32[10,10,1]{2,1,0:T(8,128)S(1)}, u32[]{:S(2)}, u32[]{:S(2)}) collective-permute-start(f32[10,10,1]{2,1,0:T(8,128)S(1)} %get-tuple-element.38), channel_id=1, source_target_pairs={{1,0},{2,1},{3,2},{5,4},{6,5},{7,6},{9,8},{10,9},{11,10},{13,12},{... | collective-permute-start | bytes 1208 | tf_op jit(solution)/shard_map/ppermute | solution.py:30
  104.1 10.4 %collective-permute-start.12 = (f32[10,1,1024]{2,1,0:T(1,128)S(1)}, f32[10,1,1024]{2,1,0:T(1,128)S(1)}, u32[]{:S(2)}, u32[]{:S(2)}) collective-permute-start(f32[10,1,1024]{2,1,0:T(1,128)S(1)} %get-tuple-element.49), channel_id=1, source_target_pairs={{4,0},{8,4},{12,8},{16,12},{20,16},{24,20},{28,24},{5,1},{9,5},{13... | collective-permute-start | bytes 122888 | tf_op jit(solution)/shard_map/ppermute | solution.py:30
  105.4 9.1 %collective-permute-start.13 = (f32[10,1,1024]{2,1,0:T(1,128)S(1)}, f32[10,1,1024]{2,1,0:T(1,128)S(1)}, u32[]{:S(2)}, u32[]{:S(2)}) collective-permute-start(f32[10,1,1024]{2,1,0:T(1,128)S(1)} %get-tuple-element.48), channel_id=1, source_target_pairs={{0,4},{4,8},{8,12},{12,16},{16,20},{20,24},{24,28},{1,5},{5,9},{9,... | collective-permute-start | bytes 122888 | tf_op jit(solution)/shard_map/ppermute | solution.py:28
  110.6 119.1 %all-to-all-start = ((s32[8,1,8]{2,1,0:T(1,128)}), s32[8,1,8]{2,1,0:T(1,128)}, u32[]{:S(2)}, u32[]{:S(2)}) async-start(s32[8,1,8]{2,1,0:T(1,128)} %bitcast), calls=%async_computation | async-start | bytes 8192 | tf_op jit(solution)/shard_map/all_to_all | solution.py:153
  114.7 3.8 %collective-permute-start.14 = (f32[10,10,1]{2,1,0:T(8,128)S(1)}, f32[10,10,1]{2,1,0:T(8,128)S(1)}, u32[]{:S(2)}, u32[]{:S(2)}) collective-permute-start(f32[10,10,1]{2,1,0:T(8,128)S(1)} %get-tuple-element.37), channel_id=1, source_target_pairs={{0,1},{1,2},{2,3},{4,5},{5,6},{6,7},{8,9},{9,10},{10,11},{12,13},{... | collective-permute-start | bytes 1208 | tf_op jit(solution)/shard_map/ppermute | solution.py:28
  116.0 5.0 %collective-permute-start.15 = (f32[10,10,1]{2,1,0:T(8,128)S(1)}, f32[10,10,1]{2,1,0:T(8,128)S(1)}, u32[]{:S(2)}, u32[]{:S(2)}) collective-permute-start(f32[10,10,1]{2,1,0:T(8,128)S(1)} %get-tuple-element.36), channel_id=1, source_target_pairs={{1,0},{2,1},{3,2},{5,4},{6,5},{7,6},{9,8},{10,9},{11,10},{13,12},{... | collective-permute-start | bytes 1208 | tf_op jit(solution)/shard_map/ppermute | solution.py:30
  161.9 7.9 %collective-permute-start.16 = (f32[10,1,1024]{2,1,0:T(1,128)S(1)}, f32[10,1,1024]{2,1,0:T(1,128)S(1)}, u32[]{:S(2)}, u32[]{:S(2)}) collective-permute-start(f32[10,1,1024]{2,1,0:T(1,128)S(1)} %get-tuple-element.47), channel_id=1, source_target_pairs={{4,0},{8,4},{12,8},{16,12},{20,16},{24,20},{28,24},{5,1},{9,5},{13... | collective-permute-start | bytes 122888 | tf_op jit(solution)/shard_map/ppermute | solution.py:30
  163.2 6.6 %collective-permute-start.17 = (f32[10,1,1024]{2,1,0:T(1,128)S(1)}, f32[10,1,1024]{2,1,0:T(1,128)S(1)}, u32[]{:S(2)}, u32[]{:S(2)}) collective-permute-start(f32[10,1,1024]{2,1,0:T(1,128)S(1)} %get-tuple-element.46), channel_id=1, source_target_pairs={{0,4},{4,8},{8,12},{12,16},{16,20},{20,24},{24,28},{1,5},{5,9},{9,... | collective-permute-start | bytes 122888 | tf_op jit(solution)/shard_map/ppermute | solution.py:28
  171.8 8.0 %collective-permute-start.18 = (f32[10,10,1]{2,1,0:T(8,128)S(1)}, f32[10,10,1]{2,1,0:T(8,128)S(1)}, u32[]{:S(2)}, u32[]{:S(2)}) collective-permute-start(f32[10,10,1]{2,1,0:T(8,128)S(1)} %get-tuple-element.35), channel_id=1, source_target_pairs={{0,1},{1,2},{2,3},{4,5},{5,6},{6,7},{8,9},{9,10},{10,11},{12,13},{... | collective-permute-start | bytes 1208 | tf_op jit(solution)/shard_map/ppermute | solution.py:28
  173.1 6.7 %collective-permute-start.19 = (f32[10,10,1]{2,1,0:T(8,128)S(1)}, f32[10,10,1]{2,1,0:T(8,128)S(1)}, u32[]{:S(2)}, u32[]{:S(2)}) collective-permute-start(f32[10,10,1]{2,1,0:T(8,128)S(1)} %get-tuple-element.34), channel_id=1, source_target_pairs={{1,0},{2,1},{3,2},{5,4},{6,5},{7,6},{9,8},{10,9},{11,10},{13,12},{... | collective-permute-start | bytes 1208 | tf_op jit(solution)/shard_map/ppermute | solution.py:30
  179.8 104.5 %copy-start = (f32[10,8,1024]{2,1,0:T(8,128)S(1)}, f32[10,8,1024]{2,1,0:T(8,128)}, u32[]{:S(2)}) copy-start(f32[10,8,1024]{2,1,0:T(8,128)} %param.21) | copy-start | bytes 983044
  220.5 7.9 %collective-permute-start.20 = (f32[10,1,1024]{2,1,0:T(1,128)S(1)}, f32[10,1,1024]{2,1,0:T(1,128)S(1)}, u32[]{:S(2)}, u32[]{:S(2)}) collective-permute-start(f32[10,1,1024]{2,1,0:T(1,128)S(1)} %get-tuple-element.45), channel_id=1, source_target_pairs={{4,0},{8,4},{12,8},{16,12},{20,16},{24,20},{28,24},{5,1},{9,5},{13... | collective-permute-start | bytes 122888 | tf_op jit(solution)/shard_map/ppermute | solution.py:30
  221.8 6.6 %collective-permute-start.21 = (f32[10,1,1024]{2,1,0:T(1,128)S(1)}, f32[10,1,1024]{2,1,0:T(1,128)S(1)}, u32[]{:S(2)}, u32[]{:S(2)}) collective-permute-start(f32[10,1,1024]{2,1,0:T(1,128)S(1)} %get-tuple-element.44), channel_id=1, source_target_pairs={{0,4},{4,8},{8,12},{12,16},{16,20},{20,24},{24,28},{1,5},{5,9},{9,... | collective-permute-start | bytes 122888 | tf_op jit(solution)/shard_map/ppermute | solution.py:28
  228.4 0.6 copy-start.11
  229.0 0.6 copy-start.12
  229.7 52.7 %all-to-all-start.1 = ((f32[8,8,1024]{2,1,0:T(8,128)}), f32[8,8,1024]{2,1,0:T(8,128)}, u32[]{:S(2)}, u32[]{:S(2)}) async-start(f32[8,8,1024]{2,1,0:T(8,128)} %convolution_bitcast_fusion), calls=%async_computation.1 | async-start | bytes 524288 | tf_op jit(solution)/shard_map/all_to_all | solution.py:152
  233.8 79.8 %all-reduce.16.cloned.1.call-start = ((), (), s32[]{:S(2)}) async-start(), calls=%async_computation.2 | async-start | bytes 262144 | tf_op jit(solution)/shard_map/psum | solution.py:164
  234.5 6.8 %collective-permute-start.22 = (f32[10,10,1]{2,1,0:T(8,128)}, f32[10,10,1]{2,1,0:T(8,128)}, u32[]{:S(2)}, u32[]{:S(2)}) collective-permute-start(f32[10,10,1]{2,1,0:T(8,128)} %get-tuple-element.33), channel_id=1, source_target_pairs={{0,1},{1,2},{2,3},{4,5},{5,6},{6,7},{8,9},{9,10},{10,11},{12,13},{... | collective-permute-start | bytes 1208 | tf_op jit(solution)/shard_map/ppermute | solution.py:28
  236.5 4.9 %collective-permute-start.23 = (f32[10,10,1]{2,1,0:T(8,128)}, f32[10,10,1]{2,1,0:T(8,128)}, u32[]{:S(2)}, u32[]{:S(2)}) collective-permute-start(f32[10,10,1]{2,1,0:T(8,128)} %get-tuple-element.32), channel_id=1, source_target_pairs={{1,0},{2,1},{3,2},{5,4},{6,5},{7,6},{9,8},{10,9},{11,10},{13,12},{... | collective-permute-start | bytes 1208 | tf_op jit(solution)/shard_map/ppermute | solution.py:30
Sparse Core Ops, SparseCore 0:
  284.4 29.0 all-reduce.15
